TPU v7x, 32 devices: a whole 2x2x4 slice. The times are simulated.
32 devices in a mesh: groups: 2 (over y), tok: 8 (over z, x), head: 2 (over core).
Axes of the slice: x: 2, y: 2, z: 4, core: 2. Of those that a mesh axis runs over, the one named last changes fastest.
Arguments:
- interior_element_embedding: bfloat16 [2048, 1024], P(('groups', 'tok')), parts along dimension 0, may hold values from -70 to 70
- boundary_element_embedding: bfloat16 [512, 1024], P(('groups', 'tok')), parts along dimension 0, may hold values from -70 to 70
- interior_landmark_position: int32 [256], P(('groups', 'tok')), parts along dimension 0, may hold values from 0 to 1023, as said below
- boundary_landmark_position: int32 [128], P(('groups', 'tok')), parts along dimension 0, may hold values from 0 to 255, as said below
- interior_rescaling_factor: float32 [1024], replicated, may hold values from 0.1 to 1.9
- boundary_rescaling_factor: float32 [1024], replicated, may hold values from 0.1 to 1.9
- question_projection_matrix: bfloat16 [1024, 1024], P(None, 'head'), may hold values from -0.1875 to 0.1875
- lookup_projection_matrix: bfloat16 [1024, 1024], P(None, 'head'), may hold values from -0.1875 to 0.1875
- content_projection_matrix: bfloat16 [1024, 1024], P(None, 'head'), may hold values from -0.1875 to 0.1875
- final_projection_matrix: bfloat16 [1024, 1024], P('head'), may hold values from -0.1875 to 0.1875
- channel_logit_divisor: float32 [16], P('head'), may hold values from 0.5 to 96
Outputs:
- update: bfloat16 [2048, 1024], P(('groups', 'tok'), 'head'), parts along dimension 0
There are 2 independent parts, one for each index of `groups`. A program takes and returns all parts, laid end to end along the dimension named above; an argument that names none is the same for every part. Nothing has to cross between parts.
Inputs may be any that keep to these rules, and one draw needn't show every extreme that they name: `interior_landmark_position`: anchor i lies among the 128 cells of block i // 16, that is from (i // 16) * 128 on; no cell is named twice; cell 0 and the last cell of the last block are always anchors. `boundary_landmark_position`: anchor i lies among the 32 cells of block i // 8, that is from (i // 8) * 32 on; no cell is named twice; cell 0 and the last cell of the last block are always anchors.
All inputs are finite; a program needn't handle non-finite values.
Results may differ from a plain program's by a relative error of at most 0.012.
The roundings to bfloat16 on the way count: a program that leaves them out, or rounds other values in their place, can miss the bound.
Values may be sent and summed in bfloat16 or wider, within the bound.
A program may use at most 64 MiB of HBM per device.

v0:
```python
import math

import jax
import jax.numpy as jnp
from jax import lax
from jax.sharding import PartitionSpec as P

epsilon = 1e-06
key_block = 512


def rms_rows(cells, gain):
    values = cells.astype(jnp.float32)
    mean_square = jnp.mean(values * values, axis=1, keepdims=True)
    return (values * lax.rsqrt(mean_square + epsilon) * gain).astype(jnp.bfloat16)


def absorb(running, key_rows, value_rows, queries, logit_multiplier):
    run_max, denominator, accumulated = running
    parallel_channel_total, channel_dimension, cell_count = queries.shape
    key_heads = key_rows.reshape(key_rows.shape[0], parallel_channel_total, channel_dimension)
    value_heads = value_rows.reshape(value_rows.shape[0], parallel_channel_total, channel_dimension)
    scores = (
        jnp.einsum("jhd,hdc->hjc", key_heads, queries, preferred_element_type=jnp.float32)
        * logit_multiplier
    )
    new_max = jnp.maximum(run_max, jnp.max(scores, axis=1))
    shrink = jnp.exp(run_max - new_max)
    exp_scores = jnp.exp(scores - new_max[:, None, :])
    denominator = denominator * shrink + jnp.sum(exp_scores, axis=1)
    added = jnp.einsum(
        "jhd,hjc->hdc",
        value_heads,
        exp_scores.astype(jnp.bfloat16),
        preferred_element_type=jnp.float32,
    )
    accumulated = accumulated * shrink[:, None, :] + added
    return (new_max, denominator, accumulated)


def make_folder(queries, logit_multiplier):

    def folder(running, shard_rows, offset):
        key_rows, value_rows = shard_rows
        row_count = key_rows.shape[0]
        if row_count > key_block and row_count % key_block == 0:
            row_width = key_rows.shape[1]

            def scan_step(state, key_pair):
                return (absorb(state, key_pair[0], key_pair[1], queries, logit_multiplier), None)

            stacked = (
                key_rows.reshape(row_count // key_block, key_block, row_width),
                value_rows.reshape(row_count // key_block, key_block, row_width),
            )
            running, unused = lax.scan(scan_step, running, stacked)
            return running
        return absorb(running, key_rows, value_rows, queries, logit_multiplier)

    return folder


def project_pair(rows_in, lookup_projection_matrix, content_projection_matrix):
    key_rows = jnp.dot(
        rows_in, lookup_projection_matrix, preferred_element_type=jnp.float32
    ).astype(jnp.bfloat16)
    value_rows = jnp.dot(
        rows_in, content_projection_matrix, preferred_element_type=jnp.float32
    ).astype(jnp.bfloat16)
    return (key_rows, value_rows)


def body(
    interior_element_embedding,
    boundary_element_embedding,
    interior_landmark_position,
    boundary_landmark_position,
    interior_rescaling_factor,
    boundary_rescaling_factor,
    question_projection_matrix,
    lookup_projection_matrix,
    content_projection_matrix,
    final_projection_matrix,
    channel_logit_divisor,
):
    block_index = lax.axis_index("tok")
    vol_normed = rms_rows(interior_element_embedding, interior_rescaling_factor)
    vol_local = interior_landmark_position - block_index * interior_element_embedding.shape[0]
    surf_local = boundary_landmark_position - block_index * boundary_element_embedding.shape[0]
    vol_picked = jnp.take(vol_normed, vol_local, axis=0)
    surf_picked = rms_rows(
        jnp.take(boundary_element_embedding, surf_local, axis=0), boundary_rescaling_factor
    )
    parallel_channel_total = channel_logit_divisor.shape[0]
    local_width = question_projection_matrix.shape[1]
    channel_dimension = local_width // parallel_channel_total
    cell_count = interior_element_embedding.shape[0]
    query_cols = lax.dot_general(
        question_projection_matrix,
        vol_normed,
        (((0,), (1,)), ((), ())),
        preferred_element_type=jnp.float32,
    )
    queries = query_cols.astype(jnp.bfloat16).reshape(
        parallel_channel_total, channel_dimension, cell_count
    )
    logit_multiplier = (channel_logit_divisor * (1.0 / math.sqrt(channel_dimension)))[:, None, None]
    start_state = (
        jnp.full((parallel_channel_total, cell_count), -1e30, jnp.float32),
        jnp.zeros((parallel_channel_total, cell_count), jnp.float32),
        jnp.zeros((parallel_channel_total, channel_dimension, cell_count), jnp.float32),
    )
    folder = make_folder(queries, logit_multiplier)
    anchors = jnp.concatenate([vol_picked, surf_picked], axis=0)
    anchor_keys, anchor_values = project_pair(
        anchors, lookup_projection_matrix, content_projection_matrix
    )
    final_state = folder(
        start_state,
        (
            lax.all_gather(anchor_keys, "tok", axis=0, tiled=True),
            lax.all_gather(anchor_values, "tok", axis=0, tiled=True),
        ),
        jnp.int32(0),
    )
    run_max, denominator, accumulated = final_state
    context = (
        (accumulated / denominator[:, None, :])
        .astype(jnp.bfloat16)
        .reshape(local_width, cell_count)
    )
    head_terms = lax.dot_general(
        context,
        final_projection_matrix,
        (((0,), (0,)), ((), ())),
        preferred_element_type=jnp.float32,
    )
    full_width = head_terms.shape[1]
    share = lax.psum_scatter(
        head_terms.astype(jnp.bfloat16), "head", scatter_dimension=1, tiled=True
    ).astype(jnp.float32)
    squares = lax.psum(jnp.sum(share * share, axis=1), "head")
    return (share * lax.rsqrt(squares[:, None] / full_width + epsilon)).astype(jnp.bfloat16)


def solution(mesh):
    placed = (
        P(("groups", "tok"), None),
        P(("groups", "tok"), None),
        P(("groups", "tok")),
        P(("groups", "tok")),
        P(),
        P(),
        P(None, "head"),
        P(None, "head"),
        P(None, "head"),
        P("head", None),
        P("head"),
    )
    return jax.shard_map(
        body, mesh=mesh, in_specs=placed, out_specs=P(("groups", "tok"), "head"), check_vma=False
    )
```

profile of v0, /device:TPU:0, one launch (start us, length us, event | category | flops | bytes accessed | tf_op | source)
XLA Modules:
  0.0 101.7 jit_solution(5933496600620693102)
XLA Ops:
  6.5 0.0 copy-start
  6.5 0.0 copy-start.1
  6.5 0.0 copy-start.2
  6.5 0.0 reduce-scatter.2.cloned.1.call-start
  6.6 0.8 compare_and_fusion
  7.4 1.4 %gather_fusion.1 = bf16[8,1024]{1,0:T(8,128)(2,1)S(1)} fusion(bf16[32,1024]{1,0:T(8,128)(2,1)} %param.12, s32[1024]{0:T(1024)S(1)} %pad_clamp_fusion), kind=kCustom, calls=%fused_computation.1 | custom fusion | bytes 32800 | tf_op jit(solution)/shard_map/jit(_take)/gather | solution.py:92
  8.8 0.2 fusion.12
  9.0 0.7 compare_and_fusion.1
  9.7 1.1 %fusion.5 = f32[128]{0:T(128)S(1)} fusion(bf16[128,1024]{1,0:T(8,128)(2,1)} %param.11), kind=kLoop, calls=%fused_computation.16 | loop fusion | flops 393088 | bytes 262656 | tf_op jit(solution)/shard_map/reduce_sum | solution.py:14
  10.8 0.8 fusion.14
  11.6 0.0 copy-done.1
  11.6 0.8 fusion.7
  12.4 0.6 gather_fusion
  13.0 0.1 broadcast_select_fusion
  13.1 0.0 copy-done.2
  13.1 0.2 convolution_convert_fusion.3
  13.3 32.5 %all_gather.6 = bf16[192,512]{1,0:T(8,128)(2,1)S(1)} all-gather(bf16[24,512]{1,0:T(8,128)(2,1)S(1)} %convolution_convert_fusion.3), channel_id=1, replica_groups=mesh['groups'=2,'tok'=8,'head'=2] {'tok'}, dimensions={0}, use_global_device_ids=true | all-gather | bytes 221184 | tf_op jit(solution)/shard_map/all_gather | solution.py:121
  45.8 0.1 copy.15
  45.9 1.5 %fusion.2 = bf16[512,128]{0,1:T(8,128)(2,1)S(1)} fusion(bf16[128,1024]{1,0:T(8,128)(2,1)S(1)} %fusion.7, bf16[1024,512]{1,0:T(8,128)(2,1)} %param.17), kind=kOutput, calls=%fused_computation.8 | convolution fusion | flops 134283264 | bytes 1441792 | tf_op jit(solution)/shard_map/dot_general | solution.py:98
  47.4 0.0 copy-start.5
  47.4 0.1 copy.16
  47.6 0.5 copy-done.5
  48.1 0.0 copy-start.3
  48.1 0.4 fusion.18
  48.5 0.1 fusion.3
  48.6 0.7 copy-done.3
  49.3 0.2 convolution_convert_fusion.2
  49.6 30.6 %all_gather.7 = bf16[192,512]{1,0:T(8,128)(2,1)S(1)} all-gather(bf16[24,512]{1,0:T(8,128)(2,1)S(1)} %convolution_convert_fusion.2), channel_id=1, replica_groups=mesh['groups'=2,'tok'=8,'head'=2] {'tok'}, dimensions={0}, use_global_device_ids=true | all-gather | bytes 221184 | tf_op jit(solution)/shard_map/all_gather | solution.py:122
  80.2 0.1 copy.17
  80.3 0.3 fusion.1
  80.6 0.0 copy-done
  80.6 1.0 %convolution_convert_fusion = bf16[128,1024]{1,0:T(8,128)(2,1)} fusion(bf16[512,128]{1,0:T(8,128)(2,1)S(1)} %bitcast.18, bf16[512,1024]{1,0:T(8,128)(2,1)S(1)} %copy-done), kind=kOutput, calls=%fused_computation.3 | convolution fusion | flops 134348800 | bytes 1441792 | tf_op jit(solution)/shard_map/dot_general | solution.py:132
  81.6 0.0 reduce-scatter.2.cloned.1.call-update
  81.7 8.8 %reduce-scatter.2.cloned.1.call-done = bf16[128,512]{1,0:T(8,128)(2,1)} async-done(((bf16[128,1024]{1,0:T(8,128)(2,1)}), bf16[128,512]{1,0:T(8,128)(2,1)}) %reduce-scatter.2.cloned.1.call-update) | async-done | bytes 131088 | tf_op jit(solution)/shard_map/reduce_scatter | solution.py:139
  90.5 0.0 copy-start.4
  90.5 1.1 %fusion.10 = f32[128]{0:T(128)S(1)} fusion(bf16[128,512]{1,0:T(8,128)(2,1)} %reduce-scatter.2.cloned.1.call-done), kind=kLoop, calls=%fused_computation.22 | loop fusion | flops 196480 | bytes 131584 | tf_op jit(solution)/shard_map/reduce_sum | solution.py:142
  91.6 2.5 %psum.7 = f32[128]{0:T(128)S(1)} all-reduce(f32[128]{0:T(128)S(1)} %fusion.10), channel_id=1, replica_groups=mesh['groups'=2,'tok'=8,'head'=2] {'head'}, use_global_device_ids=true, to_apply=%region_6.7 | all-reduce | flops 128 | bytes 1024 | tf_op jit(solution)/shard_map/psum | solution.py:142
  94.1 0.0 copy-done.4
  94.1 0.7 fusion.11
  (8 shorter events, 0.1 us)
Async XLA Ops:
  6.5 74.1 %copy-start = (bf16[512,1024]{1,0:T(8,128)(2,1)S(1)}, bf16[512,1024]{1,0:T(8,128)(2,1)}, u32[]{:S(2)}) copy-start(bf16[512,1024]{1,0:T(8,128)(2,1)} %param.20) | copy-start | bytes 3145732
  6.5 5.0 %copy-start.1 = (bf16[128,1024]{1,0:T(8,128)(2,1)S(1)}, bf16[128,1024]{1,0:T(8,128)(2,1)}, u32[]{:S(2)}) copy-start(bf16[128,1024]{1,0:T(8,128)(2,1)} %param.11) | copy-start | bytes 786436
  6.5 6.5 %copy-start.2 = (bf16[1024,512]{1,0:T(8,128)(2,1)S(1)}, bf16[1024,512]{1,0:T(8,128)(2,1)}, u32[]{:S(2)}) copy-start(bf16[1024,512]{1,0:T(8,128)(2,1)} %param.18) | copy-start | bytes 3145732
  6.5 83.9 %reduce-scatter.2.cloned.1.call-start = ((), (), s32[]{:S(2)}) async-start(), calls=%async_computation.1 | async-start | bytes 393216 | tf_op jit(solution)/shard_map/reduce_scatter | solution.py:139
  47.4 0.7 copy-start.5
  48.1 1.2 %copy-start.3 = (bf16[1024,512]{1,0:T(8,128)(2,1)S(1)}, bf16[1024,512]{1,0:T(8,128)(2,1)}, u32[]{:S(2)}) copy-start(bf16[1024,512]{1,0:T(8,128)(2,1)} %param.19) | copy-start | bytes 3145732
  90.5 3.6 %copy-start.4 = (bf16[128,512]{1,0:T(8,128)(2,1)S(1)}, bf16[128,512]{1,0:T(8,128)(2,1)}, u32[]{:S(2)}) copy-start(bf16[128,512]{1,0:T(8,128)(2,1)} %reduce-scatter.2.cloned.1.call-done) | copy-start | bytes 393220
Sparse Core Ops, SparseCore 0:
  81.8 8.6 reduce-scatter.1
where the time goes:
time: 102 us
  blocking collectives  65.6 us (64%)
  between operations  13.5 us (13%)
  waiting for transfers between devices  8.84 us (9%)
  other arithmetic  6.43 us (6%)
  local copies, waits for them, and re-layouts  3.66 us (4%)
  matrix products  3.66 us (4%)
    all_gather x1, blocking collectives, body(): lax.all_gather(anchor_keys, 'tok', axis=0, tiled=True)  32.5 us
    all_gather x1, blocking collectives, body(): lax.all_gather(anchor_values, 'tok', axis=0, tiled=True)  30.6 us
    reduce_scatter x1, waiting for transfers between devices, body(): lax.psum_scatter(head_terms.astype(jnp.bfloat16), 'head', scatter_dimensi...  8.82 us
    psum x1, blocking collectives, body(): squares = lax.psum(jnp.sum(share * share, axis=1), 'head')  2.47 us
  transfers between devices with their start and end apart: 1, of which 1 were waited for; matrix products, arithmetic and copies ran while one was open for 0% of the time, Pallas kernels for 0%

commit v1 on v0

v1 whole, which is shorter than its diff:
```python
import functools
import math

import jax
import jax.numpy as jnp
from jax import lax
from jax.experimental import pallas as pl
from jax.experimental.pallas import tpu as pltpu
from jax.sharding import PartitionSpec as P

epsilon = 1e-06
f32 = jnp.float32
bf16 = jnp.bfloat16


def repeat(count, step):
    if count <= 8:
        for number in range(count):
            step(number)
    else:
        pl.loop(0, count)(step)


def normed(values, gain):
    mean_square = jnp.mean(values * values, axis=1, keepdims=True)
    return (values * lax.rsqrt(mean_square + epsilon) * gain).astype(bf16)


def picked(positions, rows):
    lines = lax.broadcasted_iota(jnp.int32, (rows.shape[0], positions.shape[1]), 0)
    chosen = jnp.where(lines == positions, 1.0, 0.0).astype(bf16)
    return lax.dot_general(
        chosen, rows, (((0,), (0,)), ((), ())), preferred_element_type=f32
    )


def kernel(
    sizes,
    x_hbm,
    surf_hbm,
    vol_pos_hbm,
    surf_pos_hbm,
    vol_gain_hbm,
    surf_gain_hbm,
    wq_hbm,
    wk_hbm,
    wv_hbm,
    wo_hbm,
    scale_hbm,
    out_ref,
    x,
    surf,
    vol_pos,
    surf_pos,
    vol_gain,
    surf_gain,
    wq,
    wk,
    wv,
    wo,
    scale,
    gathered,
    keys,
    values,
    context,
    load_sem,
    major_send,
    minor_send,
    mate_send,
    net_recv,
    mate_recv,
    wo_send,
    wo_recv,
    ctx_send,
    ctx_recv,
):
    tok_count, minor = sizes
    major = tok_count // minor
    me = lax.axis_index("tok")
    core = lax.axis_index("head")
    mate = 1 - core
    row = me // minor
    column = me % minor
    width = x.shape[1]
    half = width // 2
    cells = x.shape[0]
    local_width = wq.shape[1]
    heads = scale.shape[1]
    head_dim = local_width // heads
    pair_width = 2 * head_dim
    pairs = heads // 2

    sources = (
        (x_hbm, x),
        (vol_pos_hbm, vol_pos),
        (surf_hbm, surf),
        (surf_pos_hbm, surf_pos),
        (vol_gain_hbm, vol_gain),
        (surf_gain_hbm, surf_gain),
        (wq_hbm, wq),
        (wk_hbm, wk),
        (wv_hbm, wv),
        (scale_hbm, scale),
    )
    loads = [
        pltpu.make_async_copy(source, target, load_sem.at[number])
        for number, (source, target) in enumerate(sources)
    ]
    for part in range(2):
        loads.append(
            pltpu.make_async_copy(
                wo_hbm.at[:, pl.ds(part * half, half)],
                wo.at[0, part],
                load_sem.at[len(sources) + part],
            )
        )
    for load in loads:
        load.start()

    side = (2 * row) // major

    def far_first(number):
        step = (major - 1 - number) * (1 - side) + (number + 1) * side
        return ((row + step) % major) * minor + column

    def near_first(number):
        step = (number + 1) * (1 - side) + (major - 1 - number) * side
        return ((row + step) % major) * minor + column

    def across(number):
        return row * minor + (column + 1 + number) % minor

    barrier = pltpu.get_barrier_semaphore()
    pl.semaphore_signal(barrier, inc=1, device_id={"head": mate})
    repeat(
        minor - 1,
        lambda number: pl.semaphore_signal(barrier, inc=1, device_id={"tok": across(number)}),
    )
    repeat(
        major - 1,
        lambda number: pl.semaphore_signal(barrier, inc=1, device_id={"tok": far_first(number)}),
    )

    for number in range(6):
        loads[number].wait()
    vol_anchor = normed(picked(vol_pos[...] - me * cells, x[...]), vol_gain[...])
    surf_anchor = normed(picked(surf_pos[...] - me * surf.shape[0], surf[...]), surf_gain[...])
    own = jnp.concatenate([vol_anchor.astype(f32), surf_anchor.astype(f32)], axis=0).astype(bf16)
    gathered[0, me] = own[:, :half]
    gathered[1, me] = own[:, half:]

    pl.semaphore_wait(barrier, major + minor - 1)

    def net_copy(source, send_sem, target):
        return pltpu.make_async_remote_copy(
            src_ref=gathered.at[core, source],
            dst_ref=gathered.at[core, source],
            send_sem=send_sem,
            recv_sem=net_recv.at[source],
            device_id={"tok": target},
        )

    def mate_copy(side_index, source):
        return pltpu.make_async_remote_copy(
            src_ref=gathered.at[side_index, source],
            dst_ref=gathered.at[side_index, source],
            send_sem=mate_send.at[source],
            recv_sem=mate_recv.at[source],
            device_id={"head": mate},
        )

    repeat(
        major - 1,
        lambda number: net_copy(me, major_send.at[number], far_first(number)).start(),
    )
    repeat(
        minor - 1,
        lambda number: net_copy(me, minor_send.at[row], across(number)).start(),
    )
    wo_copies = [
        pltpu.make_async_remote_copy(
            src_ref=wo_hbm.at[:, pl.ds(part * half, half)],
            dst_ref=wo.at[1, part],
            send_sem=wo_send.at[part],
            recv_sem=wo_recv.at[part],
            device_id={"head": mate},
        )
        for part in range(2)
    ]
    for copy in wo_copies:
        copy.start()

    cells_normed = normed(x[...].astype(f32), vol_gain[...])
    loads[6].wait()
    queries = jnp.dot(cells_normed, wq[...], preferred_element_type=f32).astype(bf16)

    def from_across(number):
        source = across(number)
        net_copy(source, minor_send.at[row], source).wait_recv()
        mate_copy(core, source).start()

    repeat(minor - 1, from_across)

    def from_major(number):
        source = near_first(number)
        net_copy(source, minor_send.at[row], source).wait_recv()
        repeat(
            minor - 1,
            lambda step: net_copy(source, minor_send.at[source // minor], across(step)).start(),
        )
        mate_copy(core, source).start()

    repeat(major - 1, from_major)

    def relayed(number):
        home = near_first(number)
        source = (home // minor) * minor + (column + 1) % minor
        net_copy(source, minor_send.at[row], source).wait_recv()
        mate_copy(core, source).start()

    if minor > 1:
        repeat(major - 1, relayed)

    def from_mate(number):
        source = (me + 1 + number) % tok_count
        mate_copy(mate, source).wait_recv()

    repeat(tok_count - 1, from_mate)

    for number in (7, 8, 9):
        loads[number].wait()
    block = gathered.shape[2]
    group = math.gcd(tok_count, 8)
    groups = tok_count // group
    group_rows = group * block

    def project(number):
        def part_rows(part):
            return jnp.concatenate(
                [gathered[part, number * group + step].astype(f32) for step in range(group)],
                axis=0,
            ).astype(bf16)

        rows = jnp.concatenate([part_rows(0), part_rows(1)], axis=1)
        keys[number] = jnp.dot(rows, wk[...], preferred_element_type=f32).astype(bf16)
        values[number] = jnp.dot(rows, wv[...], preferred_element_type=f32).astype(bf16)

    repeat(groups, project)

    lane = lax.broadcasted_iota(jnp.int32, (cells, pair_width), 1)
    first = lane < head_dim
    inverse_root = 1.0 / math.sqrt(head_dim)
    ctx_copies = []
    for pair in range(pairs):
        span = slice(pair * pair_width, (pair + 1) * pair_width)
        pair_queries = queries[:, span].astype(f32)
        stacked = jnp.concatenate(
            [jnp.where(first, pair_queries, 0.0), jnp.where(first, 0.0, pair_queries)], axis=0
        ).astype(bf16)
        multiplier = jnp.concatenate(
            [
                jnp.broadcast_to(scale[0:1, 2 * pair + step : 2 * pair + step + 1], (cells, 1))
                for step in range(2)
            ],
            axis=0,
        ) * inverse_root

        def score(number):
            return (
                lax.dot_general(
                    stacked,
                    keys[number, :, span],
                    (((1,), (1,)), ((), ())),
                    preferred_element_type=f32,
                )
                * multiplier
            )

        def weigh(number, exp_scores):
            return jnp.dot(
                exp_scores.astype(bf16), values[number, :, span], preferred_element_type=f32
            )

        scores = score(0)
        row_max = jnp.max(scores, axis=1, keepdims=True)
        exp_scores = jnp.exp(scores - row_max)
        denominator = jnp.sum(exp_scores, axis=1, keepdims=True)
        total = weigh(0, exp_scores)
        if groups > 1:

            def absorb(number, state):
                row_max, denominator, total = state
                scores = score(number)
                new_max = jnp.maximum(row_max, jnp.max(scores, axis=1, keepdims=True))
                shrink = jnp.exp(row_max - new_max)
                exp_scores = jnp.exp(scores - new_max)
                denominator = denominator * shrink + jnp.sum(exp_scores, axis=1, keepdims=True)
                return new_max, denominator, total * shrink + weigh(number, exp_scores)

            row_max, denominator, total = lax.fori_loop(
                1, groups, absorb, (row_max, denominator, total)
            )
        total = total * (1.0 / denominator)
        context[0, pair] = jnp.where(first, total[:cells], total[cells:]).astype(bf16)
        ctx_copies.append(
            pltpu.make_async_remote_copy(
                src_ref=context.at[0, pair],
                dst_ref=context.at[1, pair],
                send_sem=ctx_send.at[pair],
                recv_sem=ctx_recv.at[pair],
                device_id={"head": mate},
            )
        )
        ctx_copies[-1].start()

    for number in (10, 11):
        loads[number].wait()

    def joined(which):
        return jnp.concatenate([context[which, pair] for pair in range(pairs)], axis=1)

    mine = joined(0)
    kept = jnp.dot(mine, wo[0, core], preferred_element_type=f32)
    rest = jnp.dot(mine, wo[0, mate], preferred_element_type=f32)
    for copy in wo_copies:
        copy.wait()
    for copy in ctx_copies:
        copy.wait()
    theirs = joined(1)
    kept = kept + jnp.dot(theirs, wo[1, core], preferred_element_type=f32)
    rest = rest + jnp.dot(theirs, wo[1, mate], preferred_element_type=f32)
    squares = jnp.sum(kept * kept, axis=1, keepdims=True) + jnp.sum(
        rest * rest, axis=1, keepdims=True
    )
    out_ref[...] = (kept * lax.rsqrt(squares / width + epsilon)).astype(bf16)

    repeat(
        major - 1,
        lambda number: net_copy(me, major_send.at[number], far_first(number)).wait_send(),
    )
    if minor > 1:
        repeat(
            major,
            lambda number: net_copy(me, minor_send.at[number], across(0)).wait_send(),
        )
    repeat(
        tok_count - 1,
        lambda number: mate_copy(core, (me + 1 + number) % tok_count).wait_send(),
    )


def solution(mesh):
    tok_count = mesh.shape["tok"]
    minor = 2 if tok_count % 2 == 0 and tok_count > 2 else 1

    def body(
        interior,
        boundary,
        vol_position,
        surf_position,
        vol_gain,
        surf_gain,
        wq,
        wk,
        wv,
        wo,
        scale,
    ):
        cells, width = interior.shape
        local_width = wq.shape[1]
        heads = scale.shape[0]
        pairs = heads // 2
        block = vol_position.shape[0] + surf_position.shape[0]
        group = math.gcd(tok_count, 8)
        groups = tok_count // group
        half = width // 2
        args = (
            interior,
            boundary,
            vol_position.reshape(1, -1),
            surf_position.reshape(1, -1),
            vol_gain.reshape(1, -1),
            surf_gain.reshape(1, -1),
            wq,
            wk,
            wv,
            wo,
            scale.reshape(1, -1),
        )
        held = [pltpu.VMEM(arg.shape, arg.dtype) for arg in args]
        held[9] = pltpu.VMEM((2, 2, local_width, half), bf16)
        dma = pltpu.SemaphoreType.DMA
        return pl.pallas_call(
            functools.partial(kernel, (tok_count, minor)),
            out_shape=jax.ShapeDtypeStruct((cells, width // mesh.shape["head"]), bf16),
            in_specs=[pl.BlockSpec(memory_space=pl.ANY)] * len(args),
            out_specs=pl.BlockSpec(memory_space=pltpu.VMEM),
            scratch_shapes=held
            + [
                pltpu.VMEM((2, tok_count, block, half), bf16),
                pltpu.VMEM((groups, group * block, local_width), bf16),
                pltpu.VMEM((groups, group * block, local_width), bf16),
                pltpu.VMEM((2, pairs, cells, local_width // pairs), bf16),
                dma((12,)),
                dma((tok_count // minor,)),
                dma((tok_count // minor,)),
                dma((tok_count,)),
                dma((tok_count,)),
                dma((tok_count,)),
                dma((2,)),
                dma((2,)),
                dma((pairs,)),
                dma((pairs,)),
            ],
            compiler_params=pltpu.CompilerParams(collective_id=0, has_side_effects=True),
        )(*args)

    placed = (
        P(("groups", "tok"), None),
        P(("groups", "tok"), None),
        P(("groups", "tok")),
        P(("groups", "tok")),
        P(),
        P(),
        P(None, "head"),
        P(None, "head"),
        P(None, "head"),
        P("head", None),
        P("head"),
    )
    return jax.shard_map(
        body, mesh=mesh, in_specs=placed, out_specs=P(("groups", "tok"), "head"), check_vma=False
    )
```

time: 102 us -> 18.9 us (0.19)
  blocking collectives: 65.6 us -> 0 us
  Pallas kernels: 0 us -> 17.2 us
  between operations: 13.5 us -> 0.01 us
  waiting for transfers between devices: 8.84 us -> 0 us
  other arithmetic: 6.43 us -> 0 us
  matrix products: 3.66 us -> 0 us
  local copies, waits for them, and re-layouts: 3.66 us -> 1.57 us
    all_gather x2 -> x0, blocking collectives: 63.1 us -> none  [the longest x1 32.5 us: body(): lax.all_gather(anchor_keys, 'tok', axis=0, tiled=True)]
    pallas_call x0 -> x1, Pallas kernels: none -> 17.2 us  [body(): pl.pallas_call(functools.partial(kernel, (tok_count, minor)), out_shape=j...]
    reduce_scatter x1 -> x0, waiting for transfers between devices: 8.82 us -> none  [body(): lax.psum_scatter(head_terms.astype(jnp.bfloat16), 'head', scatter_dimensi...]
    dot_general x6 -> x0, matrix products: 3.66 us -> none  [the longest x1 1.53 us: body(): lax.dot_general(question_projection_matrix, vol_normed, (((0,), (1,)), ((...]
    reduce_sum x4 -> x0, other arithmetic: 2.48 us -> none  [the longest x2 1.28 us: rms_rows(): mean_square = jnp.mean(values * values, axis=1, keepdims=True)]
    psum x1 -> x0, blocking collectives: 2.47 us -> none  [body(): squares = lax.psum(jnp.sum(share * share, axis=1), 'head')]
    convert_element_type x3 -> x0, other arithmetic: 2.34 us -> none  [the longest x2 1.59 us: rms_rows(): (values * lax.rsqrt(mean_square + epsilon) * gain).astype(jnp.bfloat16)]
    gather x2 -> x0, local copies, waits for them, and re-layouts: 2.02 us -> none  [the longest x1 1.43 us: body(): jnp.take(boundary_element_embedding, surf_local, axis=0)]
  transfers between devices with their start and end apart: 1 -> 0, of which waited for: 1 -> 0; matrix products, arithmetic and copies ran while one was open for 0% -> 0% of each run, Pallas kernels for 0% -> 0%
where the time goes in v1:
time: 18.9 us; the launch traced here: 18.8 us
  Pallas kernels  17.2 us (91%)
  local copies, waits for them, and re-layouts  1.57 us (8%)
    pallas_call x1, Pallas kernels, body(): pl.pallas_call(functools.partial(kernel, (tok_count, minor)), out_shape=j...  17.2 us
    unnamed x1, local copies, waits for them, and re-layouts  1.57 us

profile of v1, /device:TPU:0, one launch (start us, length us, event | category | flops | bytes accessed | tf_op | source)
XLA Modules:
  0.0 18.8 jit_solution(16233887091795485255)
XLA Ops:
  0.0 17.2 %shard_map.109 = bf16[128,512]{1,0:T(8,128)(2,1)} custom-call(bf16[128,1024]{1,0:T(8,128)(2,1)} %x_hbm.1, bf16[32,1024]{1,0:T(8,128)(2,1)} %surf_hbm.1, s32[1,16]{1,0:T(1,128)} %bitcast.7, s32[1,8]{1,0:T(1,128)} %bitcast.8, f32[1,1024]{1,0:T(1,128)} %bitcast.5, f32[1,1024]{1,0:T(1,128)} %bitcast.6, bf16[1024,512]{1,0:T(8,128)(2,1)} %wq_hbm.1, ...), custom_call_target="tpu_custom_call" | custom-call | tf_op jit(solution)/shard_map/pallas_call | solution.py:393
  17.2 1.6 %copy.13 = bf16[128,512]{1,0:T(8,128)(2,1)} copy(bf16[128,512]{1,0:T(8,128)(2,1)} %shard_map.109) | data formatting | bytes 262144

commit v2 on v1

--- a/solution.py
+++ b/solution.py
@@ -351,7 +351,7 @@
 
 def solution(mesh):
     tok_count = mesh.shape["tok"]
-    minor = 2 if tok_count % 2 == 0 and tok_count > 2 else 1
+    minor = 1
 
     def body(
         interior,
@@ -392,7 +392,7 @@
         dma = pltpu.SemaphoreType.DMA
         return pl.pallas_call(
             functools.partial(kernel, (tok_count, minor)),
-            out_shape=jax.ShapeDtypeStruct((cells, width // mesh.shape["head"]), bf16),
+            out_shape=pltpu.VMEM((cells, width // mesh.shape["head"]), bf16),
             in_specs=[pl.BlockSpec(memory_space=pl.ANY)] * len(args),
             out_specs=pl.BlockSpec(memory_space=pltpu.VMEM),
             scratch_shapes=held

time: 18.9 us -> 16.2 us (0.86)
  Pallas kernels: 17.2 us -> 15.3 us
  local copies, waits for them, and re-layouts: 1.57 us -> 0.66 us
    pallas_call x1, Pallas kernels: 17.2 us -> 15.3 us  [body(): pl.pallas_call(functools.partial(kernel, (tok_count, minor)), out_shape=p...]
    unnamed x1, local copies, waits for them, and re-layouts: 1.57 us -> 0.66 us
where the time goes in v2:
time: 16.2 us; the launch traced here: 16 us
  Pallas kernels  15.3 us (94%)
  local copies, waits for them, and re-layouts  0.66 us (4%)
    pallas_call x1, Pallas kernels, body(): pl.pallas_call(functools.partial(kernel, (tok_count, minor)), out_shape=p...  15.3 us
    unnamed x1, local copies, waits for them, and re-layouts  0.66 us

profile of v2, /device:TPU:0, one launch (start us, length us, event | category | flops | bytes accessed | tf_op | source)
XLA Modules:
  0.0 16.0 jit_solution(17078987157148538467)
XLA Ops:
  0.0 15.3 %shard_map.109 = bf16[128,512]{1,0:T(8,128)(2,1)S(1)} custom-call(bf16[128,1024]{1,0:T(8,128)(2,1)} %x_hbm.1, bf16[32,1024]{1,0:T(8,128)(2,1)} %surf_hbm.1, s32[1,16]{1,0:T(1,128)} %bitcast.7, s32[1,8]{1,0:T(1,128)} %bitcast.8, f32[1,1024]{1,0:T(1,128)} %bitcast.5, f32[1,1024]{1,0:T(1,128)} %bitcast.6, bf16[1024,512]{1,0:T(8,128)(2,1)} %wq_hbm.1, ...), custom_call_target="tpu_custom_call" | custom-call | tf_op jit(solution)/shard_map/pallas_call | solution.py:393
  15.4 0.7 %copy.13 = bf16[128,512]{1,0:T(8,128)(2,1)} copy(bf16[128,512]{1,0:T(8,128)(2,1)S(1)} %shard_map.109) | data formatting | bytes 262144

commit v3 on v2

v3 whole, which is shorter than its diff:
```python
import functools
import math

import jax
import jax.numpy as jnp
from jax import lax
from jax.experimental import pallas as pl
from jax.experimental.pallas import tpu as pltpu
from jax.sharding import PartitionSpec as P

epsilon = 1e-06
f32 = jnp.float32
bf16 = jnp.bfloat16
GROUP = 8


def repeat(count, step):
    if count <= 8:
        for number in range(count):
            step(number)
    else:
        pl.loop(0, count)(step)


def normed(values, gain):
    mean_square = jnp.mean(values * values, axis=1, keepdims=True)
    return (values * lax.rsqrt(mean_square + epsilon) * gain).astype(bf16)


def picked(positions, rows):
    lines = lax.broadcasted_iota(jnp.int32, (rows.shape[0], positions.shape[1]), 0)
    chosen = jnp.where(lines == positions, 1.0, 0.0).astype(bf16)
    return lax.dot_general(
        chosen, rows, (((0,), (0,)), ((), ())), preferred_element_type=f32
    )


def kernel(
    sizes,
    x_hbm,
    surf_hbm,
    vol_pos_hbm,
    surf_pos_hbm,
    vol_gain_hbm,
    surf_gain_hbm,
    wq_hbm,
    wk_hbm,
    wv_hbm,
    wo_hbm,
    scale_hbm,
    out_ref,
    x,
    surf,
    vol_pos,
    surf_pos,
    vol_gain,
    surf_gain,
    wq,
    wk,
    wv,
    wo,
    scale,
    gathered,
    run_max,
    run_sum,
    run_total,
    context,
    load_sem,
    net_send,
    mate_send,
    net_recv,
    mate_recv,
    wo_send,
    wo_recv,
    ctx_send,
    ctx_recv,
):
    tok_count, minor = sizes
    major = tok_count // minor
    me = lax.axis_index("tok")
    core = lax.axis_index("head")
    mate = 1 - core
    row = me // minor
    column = me % minor
    width = x.shape[1]
    half = width // 2
    cells = x.shape[0]
    local_width = wq.shape[1]
    heads = scale.shape[1]
    head_dim = local_width // heads
    pair_width = 2 * head_dim
    pairs = heads // 2

    sources = (
        (x_hbm, x),
        (vol_pos_hbm, vol_pos),
        (surf_hbm, surf),
        (surf_pos_hbm, surf_pos),
        (vol_gain_hbm, vol_gain),
        (surf_gain_hbm, surf_gain),
        (wq_hbm, wq),
        (wk_hbm, wk),
        (wv_hbm, wv),
        (scale_hbm, scale),
    )
    loads = [
        pltpu.make_async_copy(source, target, load_sem.at[number])
        for number, (source, target) in enumerate(sources)
    ]
    for part in range(2):
        loads.append(
            pltpu.make_async_copy(
                wo_hbm.at[:, pl.ds(part * half, half)],
                wo.at[0, part],
                load_sem.at[len(sources) + part],
            )
        )
    for load in loads:
        load.start()

    side = (2 * row) // major

    def source_of(number):
        step = number // minor
        step = step * (1 - side) + (major - step) * side
        return ((row + step) % major) * minor + (column + number) % minor

    def far_first(number):
        return source_of(tok_count - 1 - number)

    def near_first(number):
        return source_of(number + 1)

    peers = tok_count - 1
    barrier = pltpu.get_barrier_semaphore()
    repeat(
        peers,
        lambda number: pl.semaphore_signal(barrier, inc=1, device_id={"tok": far_first(number)}),
    )
    pl.semaphore_signal(barrier, inc=1, device_id={"head": mate})

    for number in range(6):
        loads[number].wait()
    vol_anchor = normed(picked(vol_pos[...] - me * cells, x[...]), vol_gain[...])
    surf_anchor = normed(picked(surf_pos[...] - me * surf.shape[0], surf[...]), surf_gain[...])
    own = jnp.concatenate([vol_anchor.astype(f32), surf_anchor.astype(f32)], axis=0).astype(bf16)
    gathered[0, me] = own[:, :half]
    gathered[1, me] = own[:, half:]

    pl.semaphore_wait(barrier, peers + 1)

    def net_copy(number, source, target):
        return pltpu.make_async_remote_copy(
            src_ref=gathered.at[core, source],
            dst_ref=gathered.at[core, source],
            send_sem=net_send.at[number],
            recv_sem=net_recv.at[source],
            device_id={"tok": target},
        )

    def mate_copy(side_index, source):
        return pltpu.make_async_remote_copy(
            src_ref=gathered.at[side_index, source],
            dst_ref=gathered.at[side_index, source],
            send_sem=mate_send.at[source],
            recv_sem=mate_recv.at[source],
            device_id={"head": mate},
        )

    repeat(peers, lambda number: net_copy(number, me, far_first(number)).start())
    wo_copies = [
        pltpu.make_async_remote_copy(
            src_ref=wo_hbm.at[:, pl.ds(part * half, half)],
            dst_ref=wo.at[1, part],
            send_sem=wo_send.at[part],
            recv_sem=wo_recv.at[part],
            device_id={"head": mate},
        )
        for part in range(2)
    ]
    for copy in wo_copies:
        copy.start()

    cells_normed = normed(x[...].astype(f32), vol_gain[...])
    loads[6].wait()
    queries = jnp.dot(cells_normed, wq[...], preferred_element_type=f32).astype(bf16)

    def from_net(number):
        source = near_first(number)
        net_copy(0, source, source).wait_recv()
        mate_copy(core, source).start()

    repeat(peers, from_net)

    for number in (7, 8, 9):
        loads[number].wait()

    lane = lax.broadcasted_iota(jnp.int32, (cells, pair_width), 1)
    first = lane < head_dim
    inverse_root = 1.0 / math.sqrt(head_dim)
    stacked = []
    multipliers = []
    for pair in range(pairs):
        pair_queries = queries[:, pair * pair_width : (pair + 1) * pair_width].astype(f32)
        stacked.append(
            jnp.concatenate(
                [jnp.where(first, pair_queries, 0.0), jnp.where(first, 0.0, pair_queries)],
                axis=0,
            ).astype(bf16)
        )
        multipliers.append(
            jnp.concatenate(
                [
                    jnp.broadcast_to(
                        scale[0:1, 2 * pair + step : 2 * pair + step + 1], (cells, 1)
                    )
                    for step in range(2)
                ],
                axis=0,
            )
            * inverse_root
        )

    group = math.gcd(tok_count, GROUP)
    groups = tok_count // group

    def joined_rows(number):
        parts = [
            jnp.concatenate(
                [
                    gathered[part, source_of(number * group + step)].astype(f32)
                    for step in range(group)
                ],
                axis=0,
            ).astype(bf16)
            for part in range(2)
        ]
        return jnp.concatenate(parts, axis=1)

    def fold(number, finish):
        rows = joined_rows(number)
        keys = jnp.dot(rows, wk[...], preferred_element_type=f32).astype(bf16)
        values = jnp.dot(rows, wv[...], preferred_element_type=f32).astype(bf16)
        started = not (isinstance(number, int) and number == 0)
        for pair in range(pairs):
            span = slice(pair * pair_width, (pair + 1) * pair_width)
            scores = (
                lax.dot_general(
                    stacked[pair],
                    keys[:, span],
                    (((1,), (1,)), ((), ())),
                    preferred_element_type=f32,
                )
                * multipliers[pair]
            )
            row_max = jnp.max(scores, axis=1, keepdims=True)
            if started:
                row_max = jnp.maximum(row_max, run_max[pair])
            exp_scores = jnp.exp(scores - row_max)
            denominator = jnp.sum(exp_scores, axis=1, keepdims=True)
            total = jnp.dot(
                exp_scores.astype(bf16), values[:, span], preferred_element_type=f32
            )
            if started:
                shrink = jnp.exp(run_max[pair] - row_max)
                denominator = denominator + run_sum[pair] * shrink
                total = total + run_total[pair] * shrink
            if finish is None:
                run_max[pair] = row_max
                run_sum[pair] = denominator
                run_total[pair] = total
            else:
                finish(pair, total * (1.0 / denominator))

    def from_mate(number):
        mate_copy(mate, source_of(number)).wait_recv()

    ctx_copies = [
        pltpu.make_async_remote_copy(
            src_ref=context.at[0, pair],
            dst_ref=context.at[1, pair],
            send_sem=ctx_send.at[pair],
            recv_sem=ctx_recv.at[pair],
            device_id={"head": mate},
        )
        for pair in range(pairs)
    ]

    def finish(pair, total):
        context[0, pair] = jnp.where(first, total[:cells], total[cells:]).astype(bf16)
        ctx_copies[pair].start()

    repeat(group - 1, lambda number: from_mate(number + 1))
    if groups > 1:
        fold(0, None)
    if groups > 2:

        def middle(number):
            repeat(group, lambda step: from_mate((number + 1) * group + step))
            fold(number + 1, None)

        pl.loop(0, groups - 2)(middle)
    if groups > 1:
        repeat(group, lambda number: from_mate((groups - 1) * group + number))
    fold(groups - 1, finish)

    for number in (10, 11):
        loads[number].wait()

    def joined(which):
        return jnp.concatenate([context[which, pair] for pair in range(pairs)], axis=1)

    mine = joined(0)
    kept = jnp.dot(mine, wo[0, core], preferred_element_type=f32)
    rest = jnp.dot(mine, wo[0, mate], preferred_element_type=f32)
    for copy in wo_copies:
        copy.wait()
    span = local_width // 2
    for part in range(2):
        chosen = range(part * pairs // 2, (part + 1) * pairs // 2)
        for pair in chosen:
            ctx_copies[pair].wait()
        theirs = jnp.concatenate([context[1, pair] for pair in chosen], axis=1)
        rows = slice(part * span, (part + 1) * span)
        kept = kept + jnp.dot(theirs, wo[1, core, rows], preferred_element_type=f32)
        rest = rest + jnp.dot(theirs, wo[1, mate, rows], preferred_element_type=f32)
    squares = jnp.sum(kept * kept, axis=1, keepdims=True) + jnp.sum(
        rest * rest, axis=1, keepdims=True
    )
    out_ref[...] = (kept * lax.rsqrt(squares / width + epsilon)).astype(bf16)

    def drain(number):
        net_copy(number, me, far_first(number)).wait_send()
        mate_copy(core, near_first(number)).wait_send()

    repeat(peers, drain)


def solution(mesh):
    tok_count = mesh.shape["tok"]
    minor = 2 if tok_count % 2 == 0 else 1

    def body(
        interior,
        boundary,
        vol_position,
        surf_position,
        vol_gain,
        surf_gain,
        wq,
        wk,
        wv,
        wo,
        scale,
    ):
        cells, width = interior.shape
        local_width = wq.shape[1]
        heads = scale.shape[0]
        pairs = heads // 2
        block = vol_position.shape[0] + surf_position.shape[0]
        half = width // 2
        args = (
            interior,
            boundary,
            vol_position.reshape(1, -1),
            surf_position.reshape(1, -1),
            vol_gain.reshape(1, -1),
            surf_gain.reshape(1, -1),
            wq,
            wk,
            wv,
            wo,
            scale.reshape(1, -1),
        )
        held = [pltpu.VMEM(arg.shape, arg.dtype) for arg in args]
        held[9] = pltpu.VMEM((2, 2, local_width, half), bf16)
        dma = pltpu.SemaphoreType.DMA
        return pl.pallas_call(
            functools.partial(kernel, (tok_count, minor)),
            out_shape=pltpu.VMEM((cells, width // mesh.shape["head"]), bf16),
            in_specs=[pl.BlockSpec(memory_space=pl.ANY)] * len(args),
            out_specs=pl.BlockSpec(memory_space=pltpu.VMEM),
            scratch_shapes=held
            + [
                pltpu.VMEM((2, tok_count, block, half), bf16),
                pltpu.VMEM((pairs, 2 * cells, 1), f32),
                pltpu.VMEM((pairs, 2 * cells, 1), f32),
                pltpu.VMEM((pairs, 2 * cells, local_width // pairs), f32),
                pltpu.VMEM((2, pairs, cells, local_width // pairs), bf16),
                dma((12,)),
                dma((tok_count,)),
                dma((tok_count,)),
                dma((tok_count,)),
                dma((tok_count,)),
                dma((2,)),
                dma((2,)),
                dma((pairs,)),
                dma((pairs,)),
            ],
            compiler_params=pltpu.CompilerParams(collective_id=0, has_side_effects=True),
        )(*args)

    placed = (
        P(("groups", "tok"), None),
        P(("groups", "tok"), None),
        P(("groups", "tok")),
        P(("groups", "tok")),
        P(),
        P(),
        P(None, "head"),
        P(None, "head"),
        P(None, "head"),
        P("head", None),
        P("head"),
    )
    return jax.shard_map(
        body, mesh=mesh, in_specs=placed, out_specs=P(("groups", "tok"), "head"), check_vma=False
    )
```

time: 16.2 us -> 15.4 us (0.951)
  Pallas kernels: 15.3 us -> 14.6 us
    pallas_call x1, Pallas kernels: 15.3 us -> 14.6 us  [body(): pl.pallas_call(functools.partial(kernel, (tok_count, minor)), out_shape=p...]
where the time goes in v3:
time: 15.4 us; the launch traced here: 15.3 us
  Pallas kernels  14.6 us (95%)
  local copies, waits for them, and re-layouts  0.66 us (4%)
    pallas_call x1, Pallas kernels, body(): pl.pallas_call(functools.partial(kernel, (tok_count, minor)), out_shape=p...  14.6 us
    unnamed x1, local copies, waits for them, and re-layouts  0.66 us

profile of v3, /device:TPU:0, one launch (start us, length us, event | category | flops | bytes accessed | tf_op | source)
XLA Modules:
  0.0 15.3 jit_solution(6281700551384052610)
XLA Ops:
  0.0 14.6 %shard_map.109 = bf16[128,512]{1,0:T(8,128)(2,1)S(1)} custom-call(bf16[128,1024]{1,0:T(8,128)(2,1)} %x_hbm.1, bf16[32,1024]{1,0:T(8,128)(2,1)} %surf_hbm.1, s32[1,16]{1,0:T(1,128)} %bitcast.7, s32[1,8]{1,0:T(1,128)} %bitcast.8, f32[1,1024]{1,0:T(1,128)} %bitcast.5, f32[1,1024]{1,0:T(1,128)} %bitcast.6, bf16[1024,512]{1,0:T(8,128)(2,1)} %wq_hbm.1, ...), custom_call_target="tpu_custom_call" | custom-call | tf_op jit(solution)/shard_map/pallas_call | solution.py:378
  14.6 0.7 %copy.13 = bf16[128,512]{1,0:T(8,128)(2,1)} copy(bf16[128,512]{1,0:T(8,128)(2,1)S(1)} %shard_map.109) | data formatting | bytes 262144
